TPU v7x, 32 devices: a whole 2x2x4 slice. The times are simulated.
32 devices in a mesh: dp: 8 (over y, x, core), tensor: 4 (over z).
Axes of the slice: x: 2, y: 2, z: 4, core: 2. Of those that a mesh axis runs over, the one named last changes fastest.
Arguments:
- tokens: bfloat16 [8192, 1024], P('dp'), may hold values from -6 to 6
- cotangent: bfloat16 [8192, 1024], P('dp'), may hold values from -6 to 6
- seq_lengths: int32 [8, 8], P('dp'), may hold values from 0 to 1024, as said below
- norm_gain: float32 [1024], replicated, may hold values from 0.5 to 1.5
- proj_gate: bfloat16 [1024, 2048], P(None, 'tensor'), may hold values from -0.1875 to 0.1875
- proj_value: bfloat16 [1024, 2048], P(None, 'tensor'), may hold values from -0.1875 to 0.1875
- proj_pair: bfloat16 [1024, 256], replicated, may hold values from -0.1875 to 0.1875
- proj_step: bfloat16 [1024, 32], P(None, 'tensor'), may hold values from -0.1875 to 0.1875
- conv_value: float32 [4, 2048], P(None, 'tensor'), may hold values from -3 to 3
- conv_value_bias: float32 [2048], P('tensor'), may hold values from -0.5 to 0.5
- conv_pair: float32 [4, 256], replicated, may hold values from -3 to 3
- conv_pair_bias: float32 [256], replicated, may hold values from -0.5 to 0.5
- step_bias: float32 [32], P('tensor'), may hold values from -4 to -1
- log_rate: float32 [32], P('tensor'), may hold values from 0 to 2.8
- skip_gain: float32 [32], P('tensor'), may hold values from 0.5 to 1.5
- gate_gain: float32 [2048], P('tensor'), may hold values from 0.5 to 1.5
- proj_out: bfloat16 [2048, 1024], P('tensor'), may hold values from -0.125 to 0.125
Outputs:
- block_out: bfloat16 [8192, 1024], P(('dp', 'tensor'))
- grad_tokens: bfloat16 [8192, 1024], P('dp')
- grad_norm_gain: float32 [1024], replicated
- grad_proj_gate: float32 [1024, 2048], P(None, 'tensor')
- grad_proj_value: float32 [1024, 2048], P(None, 'tensor')
- grad_proj_pair: float32 [1024, 256], replicated
- grad_proj_step: float32 [1024, 32], P(None, 'tensor')
- grad_conv_value: float32 [4, 2048], P(None, 'tensor')
- grad_conv_value_bias: float32 [2048], P('tensor')
- grad_conv_pair: float32 [4, 256], replicated
- grad_conv_pair_bias: float32 [256], replicated
- grad_step_bias: float32 [32], P('tensor')
- grad_log_rate: float32 [32], P('tensor')
- grad_skip_gain: float32 [32], P('tensor')
- grad_gate_gain: float32 [2048], P('tensor')
- grad_proj_out: float32 [2048, 1024], P('tensor')
Inputs may be any that keep to these rules, and one draw needn't show every extreme that they name: `seq_lengths`: row p lists the lengths of the sequences packed in order from the first of the 1024 rows of pack p; a zero is an unused slot; each row sums to at most 1024, and rows past that sum are padding.
All inputs are finite; a program needn't handle non-finite values.
Results may differ from a plain program's by a relative error of at most 0.0098.
Values sent between devices are 32-bit elements; how exact they have to be, the bound alone decides.
No kernel may reach another device: no remote copies, remote signals or barrier semaphores. Data moves between devices by JAX's collectives and lax.ppermute only.
A program may use at most 128 MiB of HBM per device.

v0:
```python
from functools import partial
import jax
import jax.numpy as jnp
from jax import lax
from jax.sharding import PartitionSpec as P

D = 1024
GROUP = 256
DI = 2048
epsilon = 1e-05
HIGHEST = lax.Precision.HIGHEST


def segment_ids(lengths_row, row_count):
    bounds = jnp.cumsum(lengths_row)
    position = jnp.arange(row_count, dtype=jnp.int32)
    segment = jnp.sum((position[:, None] >= bounds[None, :]).astype(jnp.int32), axis=1)
    live_mask = (position < bounds[-1]).astype(jnp.float32)
    return (segment, live_mask)


def conv_silu(pre_act, weight, conv_bias, segment):
    row_count = pre_act.shape[0]
    tap_count = weight.shape[0]
    summed = conv_bias[None, :] + weight[tap_count - 1][None, :] * pre_act
    for offset in range(1, tap_count):
        shifted = jnp.pad(pre_act, ((offset, 0), (0, 0)))[:row_count]
        shifted_seg = jnp.pad(segment, (offset, 0), constant_values=-1)[:row_count]
        same_seq = (shifted_seg == segment).astype(jnp.float32)
        summed = summed + weight[tap_count - 1 - offset][None, :] * shifted * same_seq[:, None]
    return jax.nn.silu(summed)


def ssd_gate(gate_pre, value_post, pair_post, step_pre, step_bias, log_rate, skip_gain, segment):
    row_count = value_post.shape[0]
    head_count = step_pre.shape[1]
    head_dim = value_post.shape[1] // head_count
    state_dim = pair_post.shape[1] // 2
    block_count = row_count // GROUP
    step_size = jax.nn.softplus(step_pre + step_bias[None, :])
    rate_per = -jnp.exp(log_rate)
    log_decay = step_size * rate_per[None, :]
    values = value_post.reshape(row_count, head_count, head_dim)
    scaled = (values * step_size[:, :, None]).reshape(block_count, GROUP, head_count, head_dim)
    cumulative = jnp.cumsum(log_decay.reshape(block_count, GROUP, head_count), axis=1)
    seg_blocks = segment.reshape(block_count, GROUP)
    b_blocks = pair_post[:, :state_dim].reshape(block_count, GROUP, state_dim)
    c_blocks = pair_post[:, state_dim:].reshape(block_count, GROUP, state_dim)
    lower_tri = jnp.arange(GROUP)[:, None] >= jnp.arange(GROUP)[None, :]
    same_seq = (seg_blocks[:, :, None] == seg_blocks[:, None, :]) & lower_tri[None]
    log_gap = cumulative[:, :, None, :] - cumulative[:, None, :, :]
    decay_mat = jnp.where(
        same_seq[..., None], jnp.exp(jnp.where(same_seq[..., None], log_gap, 0.0)), 0.0
    )
    scores = jnp.einsum("cin,cjn->cij", c_blocks, b_blocks, precision=HIGHEST)
    weights = scores[..., None] * decay_mat
    intra_out = jnp.einsum("cijh,cjhp->cihp", weights, scaled, precision=HIGHEST)
    before = jnp.concatenate([jnp.full((1,), -1, jnp.int32), seg_blocks[:-1, -1]])
    end_same = (seg_blocks == seg_blocks[:, -1:]).astype(jnp.float32)
    to_end = jnp.exp(cumulative[:, -1:, :] - cumulative) * end_same[:, :, None]
    local_states = jnp.einsum("cjh,cjn,cjhp->chnp", to_end, b_blocks, scaled, precision=HIGHEST)
    carry_in = jnp.exp(cumulative) * (seg_blocks == before[:, None]).astype(jnp.float32)[:, :, None]
    passes = (
        jnp.exp(cumulative[:, -1, :]) * (seg_blocks[:, -1] == before).astype(jnp.float32)[:, None]
    )

    def advance(state_now, inputs):
        c_block, carry_row, local_state, pass_row = inputs
        inter_out = (
            jnp.einsum("in,hnp->ihp", c_block, state_now, precision=HIGHEST) * carry_row[:, :, None]
        )
        return (local_state + pass_row[:, None, None] * state_now, inter_out)

    start_state = jnp.zeros((head_count, state_dim, head_dim), jnp.float32)
    final_state, inter_all = lax.scan(
        advance, start_state, (c_blocks, carry_in, local_states, passes)
    )
    mixed_out = (intra_out + inter_all).reshape(row_count, head_count * head_dim)
    mixed_out = mixed_out + jnp.repeat(skip_gain, head_dim)[None, :] * value_post
    return mixed_out * jax.nn.silu(gate_pre)


def mixer_rest(
    gate_pre,
    value_pre,
    pair_post,
    step_pre,
    conv_value,
    conv_value_bias,
    step_bias,
    log_rate,
    skip_gain,
    segment,
):
    value_post = conv_silu(value_pre, conv_value, conv_value_bias, segment)
    return ssd_gate(
        gate_pre, value_post, pair_post, step_pre, step_bias, log_rate, skip_gain, segment
    )


def per_device(
    tokens,
    cotangent,
    seq_lengths,
    norm_gain,
    proj_gate,
    proj_value,
    proj_pair,
    proj_step,
    conv_value,
    conv_value_bias,
    conv_pair,
    conv_pair_bias,
    step_bias,
    log_rate,
    skip_gain,
    gate_gain,
    proj_out,
):
    row_count = tokens.shape[0]
    segment, live_mask = segment_ids(seq_lengths[0], row_count)
    widened = tokens.astype(jnp.float32)
    scale_in = lax.rsqrt(jnp.mean(widened * widened, axis=1, keepdims=True) + epsilon)
    normed = (widened * scale_in * norm_gain[None, :]).astype(jnp.bfloat16)
    gate_pre = jnp.dot(normed, proj_gate, preferred_element_type=jnp.float32)
    value_pre = jnp.dot(normed, proj_value, preferred_element_type=jnp.float32)
    pair_pre = jnp.dot(normed, proj_pair, preferred_element_type=jnp.float32)
    step_pre = jnp.dot(normed, proj_step, preferred_element_type=jnp.float32)
    pair_post = conv_silu(pair_pre, conv_pair, conv_pair_bias, segment)
    rest_fn = partial(mixer_rest, segment=segment)
    gated_value, rest_back = jax.vjp(
        rest_fn,
        gate_pre,
        value_pre,
        pair_post,
        step_pre,
        conv_value,
        conv_value_bias,
        step_bias,
        log_rate,
        skip_gain,
    )
    square_sum = lax.psum(jnp.sum(gated_value * gated_value, axis=1), "tensor")
    scale_gate = lax.rsqrt(square_sum[:, None] / DI + epsilon)
    gate_out = (gated_value * scale_gate * gate_gain[None, :]).astype(jnp.bfloat16)
    share_rows = row_count // lax.axis_size("tensor")
    first_row = lax.axis_index("tensor") * share_rows
    mixed_rows = lax.psum_scatter(
        jnp.dot(gate_out, proj_out, preferred_element_type=jnp.float32),
        "tensor",
        scatter_dimension=0,
        tiled=True,
    )
    own_rows = lax.dynamic_slice_in_dim(widened, first_row, share_rows, 0)
    own_live = lax.dynamic_slice_in_dim(live_mask, first_row, share_rows, 0)
    block_out = (own_rows + mixed_rows * own_live[:, None]).astype(jnp.bfloat16)
    cot_live = jnp.where(live_mask[:, None] > 0, cotangent, jnp.zeros_like(cotangent))
    grad_proj_out = jnp.dot(gate_out.T, cot_live, preferred_element_type=jnp.float32)
    grad_gate_out = jnp.dot(cot_live, proj_out.T, preferred_element_type=jnp.float32)
    grad_gate_gain = jnp.sum(grad_gate_out * gated_value * scale_gate, axis=0)
    weighted = grad_gate_out * gate_gain[None, :]
    stat_dot = lax.psum(jnp.sum(weighted * gated_value, axis=1), "tensor")[:, None]
    grad_gated = weighted * scale_gate - gated_value * (scale_gate**3 / DI) * stat_dot
    grads_rest = rest_back(grad_gated)
    low_gate = grads_rest[0].astype(jnp.bfloat16)
    low_value = grads_rest[1].astype(jnp.bfloat16)
    low_step = grads_rest[3].astype(jnp.bfloat16)
    grad_proj_gate = jnp.dot(normed.T, low_gate, preferred_element_type=jnp.float32)
    grad_proj_value = jnp.dot(normed.T, low_value, preferred_element_type=jnp.float32)
    grad_proj_step = jnp.dot(normed.T, low_step, preferred_element_type=jnp.float32)
    grad_local = jnp.dot(low_gate, proj_gate.T, preferred_element_type=jnp.float32)
    grad_local = grad_local + jnp.dot(low_value, proj_value.T, preferred_element_type=jnp.float32)
    grad_local = grad_local + jnp.dot(low_step, proj_step.T, preferred_element_type=jnp.float32)
    pair_grad = lax.psum(grads_rest[2], "tensor")
    pair_fn = partial(conv_silu, segment=segment)
    whole_post, pair_back = jax.vjp(pair_fn, pair_pre, conv_pair, conv_pair_bias)
    grad_pair_pre, grad_conv_pair, grad_conv_pair_bias = pair_back(pair_grad)
    low_pair = grad_pair_pre.astype(jnp.bfloat16)
    grad_proj_pair = jnp.dot(normed.T, low_pair, preferred_element_type=jnp.float32)
    grad_normed = lax.psum(grad_local, "tensor")
    grad_normed = grad_normed + jnp.dot(low_pair, proj_pair.T, preferred_element_type=jnp.float32)
    grad_norm_gain = jnp.sum(grad_normed * widened * scale_in, axis=0)
    scaled_grad = grad_normed * norm_gain[None, :]
    row_dot = jnp.sum(scaled_grad * widened, axis=1, keepdims=True)
    grad_wide = scaled_grad * scale_in - widened * (scale_in**3 / D) * row_dot
    grad_tokens = (cotangent.astype(jnp.float32) + grad_wide).astype(jnp.bfloat16)
    totals = lax.psum(
        (
            grad_norm_gain,
            grad_proj_gate,
            grad_proj_value,
            grad_proj_step,
            grads_rest[4],
            grads_rest[5],
            grads_rest[6],
            grads_rest[7],
            grads_rest[8],
            grad_gate_gain,
            grad_proj_out,
            grad_proj_pair,
            grad_conv_pair,
            grad_conv_pair_bias,
        ),
        "dp",
    )
    pair_totals = (totals[11], totals[12], totals[13])
    return (
        block_out,
        grad_tokens,
        totals[0],
        totals[1],
        totals[2],
        pair_totals[0],
        totals[3],
        totals[4],
        totals[5],
        pair_totals[1],
        pair_totals[2],
        totals[6],
        totals[7],
        totals[8],
        totals[9],
        totals[10],
    )


def solution(mesh):
    return jax.shard_map(
        per_device,
        mesh=mesh,
        in_specs=(
            P("dp", None),
            P("dp", None),
            P("dp", None),
            P(),
            P(None, "tensor"),
            P(None, "tensor"),
            P(),
            P(None, "tensor"),
            P(None, "tensor"),
            P("tensor"),
            P(),
            P(),
            P("tensor"),
            P("tensor"),
            P("tensor"),
            P("tensor"),
            P("tensor", None),
        ),
        out_specs=(
            P(("dp", "tensor"), None),
            P("dp", None),
            P(),
            P(None, "tensor"),
            P(None, "tensor"),
            P(),
            P(None, "tensor"),
            P(None, "tensor"),
            P("tensor"),
            P(),
            P(),
            P("tensor"),
            P("tensor"),
            P("tensor"),
            P("tensor"),
            P("tensor", None),
        ),
        check_vma=False,
    )
```

profile of v0, /device:TPU:0, one launch (start us, length us, event | category | flops | bytes accessed | tf_op | source)
XLA Modules:
  0.0 684.8 jit_solution(3664673852586571083)
XLA Ops:
  10.6 2.1 fusion.31
  17.0 2.3 reduce-window.19
  21.1 2.9 fusion.141
  24.0 2.8 fusion.61
  28.2 2.4 reshape.353
  30.5 2.8 copy.116
  33.4 3.2 fusion.142
  36.7 1.9 fusion.97
  40.4 3.0 fusion.79
  44.6 27.7 %while.44 = (s32[]{:T(128)}, f32[8,128,64]{1,2,0:T(8,128)}, f32[4,256,8,64]{1,3,2,0:T(8,128)}, f32[4,8,128,64]{2,3,1,0:T(8,128)}, f32[4,256,8,1]{1,2,3,0:T(8,128...) while((s32[]{:T(128)}, f32[8,128,64]{1,2,0:T(8,128)}, ...), condition=%wide.region_6.7_spmd.clone, body=%wide.region_5.6_spmd.clone.sunk | while | flops 201654272 | bytes 4632367 | solution.py:75
  47.9 1.8 bitcast_add_fusion.4
  50.8 1.7 bitcast_dynamic-update-slice_fusion.10
  55.1 1.8 bitcast_add_fusion.4
  58.0 1.7 bitcast_dynamic-update-slice_fusion.10
  62.3 1.8 bitcast_add_fusion.4
  65.2 1.7 bitcast_dynamic-update-slice_fusion.10
  69.5 1.8 bitcast_add_fusion.4
  72.3 2.3 fusion.143
  75.8 10.8 %bitcast_add_fusion.2 = f32[4,256,8,64]{1,3,2,0:T(8,128)} fusion(f32[4,256,8,64]{1,3,2,0:T(8,128)S(1)} %copy-done.90, f32[4,256,8]{1,2,0:T(8,128)S(1)} %get-tuple-element.561, f32[4,256,256]{2,1,0:T(8,128)S(1)} %fusion.143, pred[4,256,256]{2,1,0:T(8,128)(4,1)S(1)} %compare_and_fusion, f32[4,256,8,64]{1,3,2,0:T(8,128)S(1)} %copy.116, ...), kind=kOutput, calls=%fused_computation.96 | convolution fusion | flops 1620049920 | bytes 7667712 | tf_op jit(solution)/shard_map/jvp(cijh,cjhp->cihp)/dot_general | solution.py:57
  86.6 3.8 copy.144
  90.5 5.3 reshape.354
  95.9 6.3 multiply_reduce_fusion.10
  102.2 13.5 %psum.126 = f32[1024]{0:T(1024)S(1)} all-reduce(f32[1024]{0:T(1024)S(1)} %get-tuple-element.558), channel_id=1, replica_groups=mesh['dp'=8,'tensor'=4] {'tensor'}, use_global_device_ids=true, to_apply=%region_8.9 | all-reduce | flops 1024 | bytes 8192 | tf_op jit(solution)/shard_map/psum | solution.py:143
  116.3 6.0 multiply_reduce_fusion.2
  122.4 8.3 %psum.127 = f32[1024]{0:T(1024)S(1)} all-reduce(f32[1024]{0:T(1024)S(1)} %get-tuple-element.477), channel_id=1, replica_groups=mesh['dp'=8,'tensor'=4] {'tensor'}, use_global_device_ids=true, to_apply=%region_11.12 | all-reduce | flops 1024 | bytes 8192 | tf_op jit(solution)/shard_map/psum | solution.py:162
  130.7 6.2 multiply_reduce_fusion.3
  136.9 2.9 copy.121
  139.8 3.3 reshape.324
  145.6 40.1 %while.45 = (s32[]{:T(128)}, f32[8,128,64]{1,2,0:T(8,128)S(1)}, f32[4,256,128]{2,1,0:T(8,128)}, f32[4,256,8]{1,2,0:T(8,128)S(1)}, f32[4,8,128,64]{2,3,1,0:T(8,12...) while((s32[]{:T(128)}, f32[8,128,64]{1,2,0:T(8,128)S(1)}, ...), condition=%wide.region_15.16_spmd.clone, body=%wide.region_12.15_spmd.clone.sunk | while | flops 403634176 | bytes 5301641 | solution.py:75
  145.6 2.1 constant_dynamic-slice_fusion.4
  155.6 2.1 constant_dynamic-slice_fusion.4
  158.5 1.7 fusion.206
  165.7 2.1 constant_dynamic-slice_fusion.4
  175.7 2.1 constant_dynamic-slice_fusion.4
  186.3 6.5 fusion.82
  192.8 3.3 multiply_reduce_fusion.1
  196.1 3.0 copy.127
  199.0 14.8 %fusion.30 = (f32[4,256,8]{1,2,0:T(8,128)}, f32[4,256,8]{1,2,0:T(8,128)}, f32[4,256,256]{2,1,0:T(8,128)S(1)}) fusion(f32[4,256,8]{1,2,0:T(8,128)S(1)} %get-tuple-element.561, f32[4,256,256]{2,1,0:T(8,128)} %copy-done.36, pred[4,256,256]{2,1,0:T(8,128)(4,1)S(1)} %copy-done.40, f32[4,256,8,64]{1,3,2,0:T(8,128)S(1)} %copy-done.4, ...), kind=kOutput, calls=%fused_computation.55 | convolution fusion | flops 1633927168 | bytes 6684672 | tf_op jit(solution)/shard_map/transpose(jvp(cijh,cjhp->cihp))/dot_general | solution.py:57
  213.9 3.0 convolution_add_fusion.2
  216.9 2.7 convolution_add_fusion.1
  225.9 10.6 %reduce-window.21 = f32[4,8,2,128]{3,1,2,0:T(8,128)S(1)} reduce-window(f32[4,8,2,128]{3,1,2,0:T(8,128)} %add_bitcast_fusion, f32[]{:T(128)} %constant.146.clone.1), window={size=1x1x1x128 pad=0_0x0_0x0_0x0_127}, to_apply=%region_20.21 | reduce-window | flops 1040384 | bytes 65540 | tf_op jit(solution)/shard_map/reduce-window.3
  238.6 9.9 %bitcast_add_fusion.1 = f32[4,256,8,64]{1,3,2,0:T(8,128)} fusion(f32[4,256,8,64]{1,3,2,0:T(8,128)} %get-tuple-element.603, f32[4,256,8]{1,2,0:T(8,128)S(1)} %get-tuple-element.561, f32[4,256,256]{2,1,0:T(8,128)} %copy-done.36, pred[4,256,256]{2,1,0:T(8,128)(4,1)S(1)} %copy-done.40, f32[4,8,64,256]{3,0,2,1:T(4,128)S(1)} %bitcast.248, ...), kind=kOutput, calls=%fused_computation.95 | convolution fusion | flops 1620049920 | bytes 7667712 | tf_op jit(solution)/shard_map/transpose(jvp(cijh,cjhp->cihp))/dot_general | solution.py:57
  248.5 4.0 copy.145
  254.1 4.8 reshape.355
  260.5 3.1 copy.126
  263.6 7.2 %multiply_reduce_fusion.7 = (f32[512]{0:T(512)S(1)}, f32[512]{0:T(512)S(1)}, f32[512]{0:T(512)S(1)}, f32[512]{0:T(512)S(1)}, f32[512]{0:T(512)S(1)}, /*index=5*/f32[1024,512]{1,0:T(8,128)S(1)}) fusion(f32[1024,512]{1,0:T(8,128)} %copy-done.21, f32[1024]{0:T(1024)S(1)} %get-tuple-element.598, f32[1024]{0:T(1024)S(1)} %get-tuple-element.597, ...), kind=kLoop, calls=%fused_computation.103 | loop fusion | flops 12580352 | bytes 12607488 | tf_op jit(solution)/shard_map/transpose(jvp())/reduce_sum | solution.py:30
  278.9 2.7 add_add_fusion
  283.3 4.9 fusion.130
  289.7 3.9 fusion.147
  293.7 2.6 fusion.146
  296.3 2.8 fusion.102
  299.1 171.3 %all-reduce.35.cloned.1.call-done = (f32[1024,1024]{1,0:T(8,128)}, f32[1024,256]{1,0:T(8,128)}) async-done(((f32[1024,1024]{1,0:T(8,128)}, f32[1024,256]{1,0:T(8,128)}), (f32[1024,1024]{1,0:T(8,128)}, f32[1024,256]{1,0:T(8,128)})) %all-reduce.35.cloned.1.call-update) | async-done | bytes 5242896 | tf_op jit(solution)/shard_map/psum | solution.py:180
  470.4 3.9 multiply_reduce_fusion.14
  476.2 1.7 fusion.148
  478.0 1.7 copy-done.2
  479.7 2.4 convert_element_type.89
  483.2 2.0 fusion.110
  485.2 5.6 fusion.40
  490.8 26.2 %all-reduce.27 = (f32[1024]{0:T(1024)}, f32[1024,8]{0,1:T(8,128)}, f32[4,512]{1,0:T(4,128)}, f32[512]{0:T(512)}, f32[4,256]{1,0:T(4,128)}, /*index=5*/f32[256]{0...) all-reduce(f32[1024]{0:T(1024)S(1)} %get-tuple-element.474, ...), channel_id=1, replica_groups=mesh['dp'=8,'tensor'=4] {'dp'}, use_global_device_ids=true, to_apply=%region_27.28 | all-reduce | flops 13592 | bytes 108736 | tf_op jit(solution)/shard_map/psum | solution.py:187
  517.1 4.6 fusion.37
  521.7 26.8 %reduce-scatter.2.cloned.1.call-done = f32[256,1024]{1,0:T(8,128)} async-done(((f32[1024,1024]{1,0:T(8,128)}), f32[256,1024]{1,0:T(8,128)}) %reduce-scatter.2.cloned.1.call-update) | async-done | bytes 1048592 | tf_op jit(solution)/shard_map/reduce_scatter | solution.py:148
  548.5 2.5 add_convert_fusion
  551.0 118.4 %all-reduce.33.cloned.1.call-done = (f32[1024,512]{1,0:T(8,128)}, f32[1024,512]{1,0:T(8,128)}, f32[1024,256]{1,0:T(8,128)}, f32[512,1024]{1,0:T(8,128)}) async-done(((f32[1024,512]{1,0:T(8,128)}, f32[1024,512]{1,0:T(8,128)}, f32[1024,256]{1,0:T(8,128)}, f32[512,1024]{1,0:T(8,128)}), (f32[1024,512]{1,0:T(8,128)}, f32[1024,512]{1,0:T(8,128)}, f32[1024,256]{1,0:T(8,128)}, ...) | async-done | bytes 7340048 | tf_op jit(solution)/shard_map/psum | solution.py:187
  669.4 3.2 copy.229
  (339 shorter events, 95.1 us)
Async XLA Ops:
  7.2 88.7 %copy-start = (bf16[1024,512]{1,0:T(8,128)(2,1)S(1)}, bf16[1024,512]{1,0:T(8,128)(2,1)}, u32[]{:S(2)}) copy-start(bf16[1024,512]{1,0:T(8,128)(2,1)} %param.25) | copy-start | bytes 3145732
  7.2 6.7 copy-start.1
  7.2 6.1 copy-start.93
  7.2 6.7 copy-start.53
  7.2 463.2 %all-reduce.35.cloned.1.call-start = ((), (), s32[]{:S(2)}) async-start(), calls=%async_computation.3 | async-start | bytes 10485760 | tf_op jit(solution)/shard_map/psum | solution.py:180
  15.8 5.3 copy-start.91
  20.3 3.7 copy-start.55
  21.1 2.9 copy-start.78
  21.1 3.0 copy-start.82
  23.9 2.9 copy-start.21
  24.0 2.8 copy-start.56
  33.4 41.6 %copy-start.3 = (f32[4,256,8,64]{1,3,2,0:T(8,128)}, f32[4,256,8,64]{1,3,2,0:T(8,128)S(1)}, u32[]{:S(2)}) copy-start(f32[4,256,8,64]{1,3,2,0:T(8,128)S(1)} %copy.116) | copy-start | bytes 6291460
  33.4 3.2 copy-start.81
  33.4 3.2 copy-start.87
  36.6 2.9 copy-start.24
  36.6 2.9 copy-start.69
  36.6 2.8 copy-start.71
  36.6 2.8 copy-start.73
  36.6 2.8 copy-start.75
  36.7 2.8 copy-start.45
  36.7 2.9 copy-start.79
  39.5 5.1 copy-start.12
  44.6 3.3 copy-start.84
  50.8 4.3 copy-start.84
  58.0 4.3 copy-start.84
  65.2 4.3 copy-start.84
  72.3 3.5 copy-start.90
  90.5 5.3 copy-start.88
  90.5 5.4 copy-start.7
  95.9 34.8 %copy-start.66 = (f32[512]{0:T(512)}, f32[512]{0:T(512)S(1)}, u32[]{:S(2)}) copy-start(f32[512]{0:T(512)S(1)} %mul.754) | copy-start | bytes 6148
  95.9 20.4 %copy-start.64 = (f32[512]{0:T(512)S(1)}, f32[512]{0:T(512)}, u32[]{:S(2)}) copy-start(f32[512]{0:T(512)} %param.36) | copy-start | bytes 6148
  116.3 6.1 copy-start.95
  116.3 14.4 %copy-start.9 = (f32[1024,512]{1,0:T(8,128)S(1)}, f32[1024,512]{1,0:T(8,128)}, u32[]{:S(2)}) copy-start(f32[1024,512]{1,0:T(8,128)} %get-tuple-element.563) | copy-start | bytes 6291460
  139.8 5.8 copy-start.17
  185.7 7.1 %copy-start.4 = (f32[4,256,8,64]{1,3,2,0:T(8,128)S(1)}, f32[4,256,8,64]{1,3,2,0:T(8,128)}, u32[]{:S(2)}) copy-start(f32[4,256,8,64]{1,3,2,0:T(8,128)} %copy-done.3) | copy-start | bytes 6291460
  185.7 7.1 %copy-start.13 = (f32[1024,128]{1,0:T(8,128)S(1)}, f32[1024,128]{1,0:T(8,128)}, u32[]{:S(2)}) copy-start(f32[1024,128]{1,0:T(8,128)} %copy-done.12) | copy-start | bytes 1572868
  185.7 7.1 %copy-start.19 = (f32[4,8,128,64]{2,3,1,0:T(8,128)S(1)}, f32[4,8,128,64]{2,3,1,0:T(8,128)}, u32[]{:S(2)}) copy-start(f32[4,8,128,64]{2,3,1,0:T(8,128)} %get-tuple-element.321) | copy-start | bytes 3145732
  196.1 3.0 copy-start.40
  199.0 14.9 %copy-start.14 = (f32[1024,128]{1,0:T(8,128)S(1)}, f32[1024,128]{1,0:T(8,128)}, u32[]{:S(2)}) copy-start(f32[1024,128]{1,0:T(8,128)} %copy-done.12) | copy-start | bytes 1572868
  213.9 3.0 copy-start.11
  213.9 3.0 copy-start.28
  213.9 5.7 copy-start.46
  213.9 5.7 copy-start.52
  216.9 21.7 %copy-start.18 = (f32[4,256,8,64]{1,0,3,2:T(4,128)S(1)}, f32[4,256,8,64]{1,0,3,2:T(4,128)}, u32[]{:S(2)}) copy-start(f32[4,256,8,64]{1,0,3,2:T(4,128)} %get-tuple-element.875) | copy-start | bytes 6291460
  248.5 4.0 copy-start.20
  260.5 3.1 copy-start.10
  260.5 3.1 copy-start.67
  263.6 7.3 %copy-start.59 = (f32[1,512]{1,0:T(1,128)S(1)}, f32[1,512]{1,0:T(1,128)}, u32[]{:S(2)}) copy-start(f32[1,512]{1,0:T(1,128)} %copy-done.58) | copy-start | bytes 6148
  263.6 7.3 %copy-start.61 = (f32[1,512]{1,0:T(1,128)S(1)}, f32[1,512]{1,0:T(1,128)}, u32[]{:S(2)}) copy-start(f32[1,512]{1,0:T(1,128)} %copy-done.60) | copy-start | bytes 6148
  263.6 7.3 %copy-start.63 = (f32[1,512]{1,0:T(1,128)S(1)}, f32[1,512]{1,0:T(1,128)}, u32[]{:S(2)}) copy-start(f32[1,512]{1,0:T(1,128)} %copy-done.62) | copy-start | bytes 6148
  281.7 266.8 %reduce-scatter.2.cloned.1.call-start = ((), (), s32[]{:S(2)}) async-start(), calls=%async_computation.1 | async-start | bytes 5242880 | tf_op jit(solution)/shard_map/reduce_scatter | solution.py:148
  288.2 381.2 %all-reduce.33.cloned.1.call-start = ((), (), s32[]{:S(2)}) async-start(), calls=%async_computation.2 | async-start | bytes 14680064 | tf_op jit(solution)/shard_map/psum | solution.py:187
  289.7 3.9 copy-start.34
  470.4 3.9 copy-start.72
  470.4 3.9 copy-start.74
  470.4 4.0 copy-start.76
  479.7 3.5 copy-start.94
  482.1 3.1 copy-start.48
  482.1 3.1 copy-start.54
  482.3 2.9 copy-start.27
  482.3 2.9 copy-start.38
  485.2 5.6 copy-start.83
  485.2 31.8 %copy-start.68 = (f32[1024]{0:T(1024)S(1)}, f32[1024]{0:T(1024)}, u32[]{:S(2)}) copy-start(f32[1024]{0:T(1024)} %get-tuple-element.584) | copy-start | bytes 12292
  669.4 3.2 copy-start.30
  (39 other events, 62.5 us)
Sparse Core Ops, SparseCore 0:
  281.8 188.5 all-reduce.34
  472.7 75.7 reduce-scatter.1
  553.2 116.0 all-reduce.32
where the time goes:
time: 696 us; the launch traced here: 685 us
  waiting for transfers between devices  317 us (46%)
  matrix products  124 us (18%)
  local copies, waits for them, and re-layouts  93.4 us (13%)
  other arithmetic  87.7 us (13%)
  blocking collectives  48 us (7%)
  between operations  15.1 us (2%)
    psum x1, waiting for transfers between devices, per_device(): grad_normed = lax.psum(grad_local, 'tensor')  171 us
    psum x1, waiting for transfers between devices, per_device(): lax.psum((grad_norm_gain, grad_proj_gate, grad_proj_value, grad_proj_step...  118 us
    dot_general x3, matrix products, ssd_gate(): jnp.einsum('cijh,cjhp->cihp', weights, scaled, precision=HIGHEST)  35.6 us
    reduce_scatter x1, waiting for transfers between devices, per_device(): lax.psum_scatter(jnp.dot(gate_out, proj_out, preferred_element_type=jnp.f...  26.8 us
    psum x1, blocking collectives, per_device(): lax.psum((grad_norm_gain, grad_proj_gate, grad_proj_value, grad_proj_step...  26.2 us
    unnamed x196, local copies, waits for them, and re-layouts  20.6 us
    another operation x9, other arithmetic  16.7 us
  transfers between devices with their start and end apart: 3, of which 3 were waited for; matrix products, arithmetic and copies ran while one was open for 6% of the time, Pallas kernels for 0%

commit v1 on v0

--- a/solution.py
+++ b/solution.py
@@ -9,6 +9,10 @@
 DI = 2048
 epsilon = 1e-05
 HIGHEST = lax.Precision.HIGHEST
+
+
+def _do_page(array_here):
+    return jnp.sum(jax.lax.all_gather(array_here, axis_name="tensor"), axis=0)
 
 
 def segment_ids(lengths_row, row_count):
@@ -177,7 +181,7 @@
     grad_pair_pre, grad_conv_pair, grad_conv_pair_bias = pair_back(pair_grad)
     low_pair = grad_pair_pre.astype(jnp.bfloat16)
     grad_proj_pair = jnp.dot(normed.T, low_pair, preferred_element_type=jnp.float32)
-    grad_normed = lax.psum(grad_local, "tensor")
+    grad_normed = _do_page(grad_local)
     grad_normed = grad_normed + jnp.dot(low_pair, proj_pair.T, preferred_element_type=jnp.float32)
     grad_norm_gain = jnp.sum(grad_normed * widened * scale_in, axis=0)
     scaled_grad = grad_normed * norm_gain[None, :]

time: 696 us -> 775 us (1.11)
  waiting for transfers between devices: 317 us -> 403 us
  local copies, waits for them, and re-layouts: 93.4 us -> 82.3 us
    all_gather x0 -> x1, waiting for transfers between devices: none -> 286 us  [_do_page(): return jnp.sum(jax.lax.all_gather(array_here, axis_name='tensor'), axis=0)]
    psum x1, waiting for transfers between devices: 171 us -> 0.01 us  [per_device(): pair_grad = lax.psum(grads_rest[2], 'tensor')]
    psum x1, waiting for transfers between devices: 118 us -> 71.6 us  [per_device(): lax.psum((grad_norm_gain, grad_proj_gate, grad_proj_value, grad_proj_step...]
    reduce_scatter x1, waiting for transfers between devices: 26.8 us -> 44.9 us  [per_device(): lax.psum_scatter(jnp.dot(gate_out, proj_out, preferred_element_type=jnp.f...]
    reduce_sum x0 -> x1, other arithmetic: none -> 10.3 us  [_do_page(): return jnp.sum(jax.lax.all_gather(array_here, axis_name='tensor'), axis=0)]
    unnamed x196 -> x204, local copies, waits for them, and re-layouts: 20.6 us -> 19.7 us
  transfers between devices with their start and end apart: 3 -> 4, of which waited for: 3 -> 3; matrix products, arithmetic and copies ran while one was open for 6% -> 13% of each run, Pallas kernels for 0% -> 0%
where the time goes in v1:
time: 775 us; the launch traced here: 763 us
  waiting for transfers between devices  403 us (52%)
  matrix products  120 us (15%)
  other arithmetic  93.1 us (12%)
  local copies, waits for them, and re-layouts  82.3 us (11%)
  blocking collectives  49.1 us (6%)
  between operations  15.4 us (2%)
    all_gather x1, waiting for transfers between devices, _do_page(): return jnp.sum(jax.lax.all_gather(array_here, axis_name='tensor'), axis=0)  286 us
    psum x1, waiting for transfers between devices, per_device(): lax.psum((grad_norm_gain, grad_proj_gate, grad_proj_value, grad_proj_step...  71.6 us
    reduce_scatter x1, waiting for transfers between devices, per_device(): lax.psum_scatter(jnp.dot(gate_out, proj_out, preferred_element_type=jnp.f...  44.9 us
    dot_general x3, matrix products, ssd_gate(): jnp.einsum('cijh,cjhp->cihp', weights, scaled, precision=HIGHEST)  33.7 us
    psum x1, blocking collectives, per_device(): lax.psum((grad_norm_gain, grad_proj_gate, grad_proj_value, grad_proj_step...  27.3 us
    unnamed x204, local copies, waits for them, and re-layouts  19.7 us
  transfers between devices with their start and end apart: 4, of which 3 were waited for; matrix products, arithmetic and copies ran while one was open for 13% of the time, Pallas kernels for 0%

profile of v1, /device:TPU:0, one launch (start us, length us, event | category | flops | bytes accessed | tf_op | source)
XLA Modules:
  0.0 763.2 jit_solution(1655553466612101974)
XLA Ops:
  10.6 2.1 fusion.31
  17.1 2.3 reduce-window.19
  21.1 2.9 fusion.141
  24.1 2.8 fusion.61
  28.2 2.4 reshape.354
  30.6 2.8 copy.116
  33.4 3.2 fusion.142
  36.7 1.9 fusion.97
  40.5 3.1 fusion.79
  44.7 27.7 %while.44 = (s32[]{:T(128)}, f32[8,128,64]{1,2,0:T(8,128)}, f32[4,256,8,64]{1,3,2,0:T(8,128)}, f32[4,8,128,64]{2,3,1,0:T(8,128)}, f32[4,256,8,1]{1,2,3,0:T(8,128...) while((s32[]{:T(128)}, f32[8,128,64]{1,2,0:T(8,128)}, ...), condition=%wide.region_6.7_spmd.clone, body=%wide.region_5.6_spmd.clone.sunk | while | flops 201654272 | bytes 4632367 | solution.py:79
  48.0 1.7 bitcast_add_fusion.4
  55.2 1.7 bitcast_add_fusion.4
  62.4 1.7 bitcast_add_fusion.4
  69.5 1.7 bitcast_add_fusion.4
  72.4 2.3 fusion.143
  75.8 10.8 %bitcast_add_fusion.2 = f32[4,256,8,64]{1,3,2,0:T(8,128)} fusion(f32[4,256,8,64]{1,3,2,0:T(8,128)S(1)} %copy-done.94, f32[4,256,8]{1,2,0:T(8,128)S(1)} %get-tuple-element.559, f32[4,256,256]{2,1,0:T(8,128)S(1)} %fusion.143, pred[4,256,256]{2,1,0:T(8,128)(4,1)S(1)} %compare_and_fusion, f32[4,256,8,64]{1,3,2,0:T(8,128)S(1)} %copy.116, ...), kind=kOutput, calls=%fused_computation.96 | convolution fusion | flops 1620049920 | bytes 7667712 | tf_op jit(solution)/shard_map/jvp(cijh,cjhp->cihp)/dot_general | solution.py:61
  86.7 3.8 copy.144
  90.5 5.0 reshape.355
  95.6 6.8 multiply_reduce_fusion.10
  102.4 13.5 %psum.119 = f32[1024]{0:T(1024)S(1)} all-reduce(f32[1024]{0:T(1024)S(1)} %get-tuple-element.556), channel_id=1, replica_groups=mesh['dp'=8,'tensor'=4] {'tensor'}, use_global_device_ids=true, to_apply=%region_8.9 | all-reduce | flops 1024 | bytes 8192 | tf_op jit(solution)/shard_map/psum | solution.py:147
  116.6 5.9 multiply_reduce_fusion.2
  122.5 8.3 %psum.120 = f32[1024]{0:T(1024)S(1)} all-reduce(f32[1024]{0:T(1024)S(1)} %get-tuple-element.477), channel_id=1, replica_groups=mesh['dp'=8,'tensor'=4] {'tensor'}, use_global_device_ids=true, to_apply=%region_11.12 | all-reduce | flops 1024 | bytes 8192 | tf_op jit(solution)/shard_map/psum | solution.py:166
  130.8 6.7 multiply_reduce_fusion.3
  137.5 2.9 copy.121
  140.4 3.2 reshape.324
  143.6 15.1 %fusion.30 = (f32[4,256,8]{1,2,0:T(8,128)}, f32[4,256,8]{1,2,0:T(8,128)}, f32[4,256,256]{2,1,0:T(8,128)}) fusion(f32[4,256,8]{1,2,0:T(8,128)S(1)} %get-tuple-element.559, f32[4,256,256]{2,1,0:T(8,128)} %copy-done.29, pred[4,256,256]{2,1,0:T(8,128)(4,1)} %copy-done.32, f32[4,256,8,64]{1,3,2,0:T(8,128)S(1)} %copy.116, f32[4,256,8]{1,2,0:T(8,128)S(1)} %bitcast.258, ...), kind=kOutput, calls=%fused_computation.55 | convolution fusion | flops 1633927168 | bytes 6684672 | tf_op jit(solution)/shard_map/transpose(jvp(cijh,cjhp->cihp))/dot_general | solution.py:61
  159.4 40.1 %while.45 = (s32[]{:T(128)}, f32[8,128,64]{1,2,0:T(8,128)S(1)}, f32[4,256,128]{2,1,0:T(8,128)S(1)}, f32[4,256,8]{1,2,0:T(8,128)}, f32[4,8,128,64]{2,3,1,0:T(8,12...) while((s32[]{:T(128)}, f32[8,128,64]{1,2,0:T(8,128)S(1)}, ...), condition=%wide.region_15.16_spmd.clone, body=%wide.region_12.15_spmd.clone.sunk | while | flops 403634176 | bytes 5301641 | solution.py:79
  159.4 2.1 constant_dynamic-slice_fusion.4
  162.3 1.9 fusion.206
  169.4 2.1 constant_dynamic-slice_fusion.4
  172.2 1.9 fusion.206
  179.3 2.1 constant_dynamic-slice_fusion.4
  182.1 1.9 fusion.206
  189.2 2.1 constant_dynamic-slice_fusion.4
  192.1 1.9 fusion.206
  199.6 5.5 fusion.82
  206.2 1.9 convolution_add_fusion.1
  210.1 4.5 fusion.130
  214.7 3.2 copy.127
  217.9 3.5 multiply_reduce_fusion.1
  221.5 7.8 %bitcast_add_fusion.1 = f32[4,256,8,64]{1,3,2,0:T(8,128)S(1)} fusion(f32[4,256,8,64]{1,3,2,0:T(8,128)S(1)} %get-tuple-element.601, f32[4,256,8]{1,2,0:T(8,128)S(1)} %get-tuple-element.559, f32[4,256,256]{2,1,0:T(8,128)S(1)} %copy-done.30, pred[4,256,256]{2,1,0:T(8,128)(4,1)S(1)} %copy-done.33, f32[4,8,64,256]{3,0,2,1:T(4,128)S(1)} %bitcast.250, ...), kind=kOutput, calls=%fused_computation.95 | convolution fusion | flops 1620049920 | bytes 7667712 | tf_op jit(solution)/shard_map/transpose(jvp(cijh,cjhp->cihp))/dot_general | solution.py:61
  229.3 2.8 copy.145
  232.0 4.8 reshape.356
  238.4 3.0 copy.126
  242.0 9.9 %reduce-window.21 = f32[4,8,2,128]{3,1,2,0:T(8,128)S(1)} reduce-window(f32[4,8,2,128]{3,1,2,0:T(8,128)S(1)} %add_bitcast_fusion, f32[]{:T(128)} %constant.146.clone.1), window={size=1x1x1x128 pad=0_0x0_0x0_0x0_127}, to_apply=%region_20.21 | reduce-window | flops 1040384 | bytes 65540 | tf_op jit(solution)/shard_map/reduce-window.3
  252.5 2.3 multiply_reduce_fusion.8
  256.3 4.0 multiply_reduce_fusion.7
  265.6 2.8 add_add_fusion
  268.4 1.9 copy-done.7
  270.3 3.9 fusion.147
  274.2 2.6 fusion.146
  276.8 2.8 fusion.102
  279.6 4.2 multiply_reduce_fusion.14
  289.0 2.4 convert_element_type.89
  292.4 2.0 fusion.110
  294.4 44.9 %reduce-scatter.2.cloned.1.call-done = f32[256,1024]{1,0:T(8,128)} async-done(((f32[1024,1024]{1,0:T(8,128)}), f32[256,1024]{1,0:T(8,128)}) %reduce-scatter.2.cloned.1.call-update) | async-done | bytes 1048592 | tf_op jit(solution)/shard_map/reduce_scatter | solution.py:152
  339.3 2.5 add_convert_fusion
  341.8 286.4 %all-gather.3.cloned.1.call-done = f32[4096,1024]{1,0:T(8,128)} async-done(((f32[1024,1024]{1,0:T(8,128)}), f32[4096,1024]{1,0:T(8,128)}) %all-gather.3.cloned.1.call-update) | async-done | bytes 16777232 | tf_op jit(solution)/shard_map/all_gather | solution.py:15
  628.2 10.3 %reduce_sum.292 = f32[1024,1024]{1,0:T(8,128)} reduce(f32[4,1024,1024]{2,1,0:T(8,128)} %bitcast.243, f32[]{:T(128)} %constant.146.clone.1), dimensions={0}, to_apply=%region_22.23 | reduce | flops 3145728 | bytes 20971524 | tf_op jit(solution)/shard_map/reduce_sum | solution.py:15
  638.5 5.8 fusion.40
  644.3 27.3 %all-reduce.27 = (f32[1024]{0:T(1024)}, f32[1024,8]{0,1:T(8,128)}, f32[4,512]{1,0:T(4,128)}, f32[512]{0:T(512)}, f32[4,256]{1,0:T(4,128)}, /*index=5*/f32[256]{0...) all-reduce(f32[1024]{0:T(1024)S(1)} %get-tuple-element.474, ...), channel_id=1, replica_groups=mesh['dp'=8,'tensor'=4] {'dp'}, use_global_device_ids=true, to_apply=%region_27.28 | all-reduce | flops 13592 | bytes 108736 | tf_op jit(solution)/shard_map/psum | solution.py:191
  671.6 4.5 fusion.37
  676.2 71.6 %all-reduce.34.cloned.1.call-done = (f32[1024,512]{1,0:T(8,128)}, f32[1024,512]{1,0:T(8,128)}, f32[1024,256]{1,0:T(8,128)}, f32[512,1024]{1,0:T(8,128)}) async-done(((f32[1024,512]{1,0:T(8,128)}, f32[1024,512]{1,0:T(8,128)}, f32[1024,256]{1,0:T(8,128)}, f32[512,1024]{1,0:T(8,128)}), (f32[1024,512]{1,0:T(8,128)}, f32[1024,512]{1,0:T(8,128)}, f32[1024,256]{1,0:T(8,128)}, ...) | async-done | bytes 7340048 | tf_op jit(solution)/shard_map/psum | solution.py:191
  747.8 3.2 copy.229
  (351 shorter events, 84.1 us)
Async XLA Ops:
  7.2 88.4 %copy-start = (bf16[1024,512]{1,0:T(8,128)(2,1)S(1)}, bf16[1024,512]{1,0:T(8,128)(2,1)}, u32[]{:S(2)}) copy-start(bf16[1024,512]{1,0:T(8,128)(2,1)} %param.25) | copy-start | bytes 3145732
  7.2 6.7 copy-start.1
  7.2 6.1 copy-start.97
  7.2 6.7 copy-start.51
  7.2 272.4 %all-reduce.32.cloned.1.call-start = ((), (), s32[]{:S(2)}) async-start(), calls=%async_computation.2 | async-start | bytes 2097152 | tf_op jit(solution)/shard_map/psum | solution.py:178
  8.4 31.2 %copy-start.41 = (s32[4,256]{1,0:T(4,128)}, s32[4,256]{1,0:T(4,128)S(1)}, u32[]{:S(2)}) copy-start(s32[4,256]{1,0:T(4,128)S(1)} %eq.73) | copy-start | bytes 12292
  9.4 27.3 %copy-start.35 = (f32[1024]{0:T(1024)}, f32[1024]{0:T(1024)S(1)}, u32[]{:S(2)}) copy-start(f32[1024]{0:T(1024)S(1)} %get-tuple-element.596) | copy-start | bytes 12292
  15.8 5.3 copy-start.95
  20.3 3.6 copy-start.53
  21.1 2.9 copy-start.81
  21.1 3.0 copy-start.86
  33.4 110.2 %copy-start.3 = (f32[4,256,8,64]{1,3,2,0:T(8,128)}, f32[4,256,8,64]{1,3,2,0:T(8,128)S(1)}, u32[]{:S(2)}) copy-start(f32[4,256,8,64]{1,3,2,0:T(8,128)S(1)} %copy.116) | copy-start | bytes 6291460
  33.4 3.2 copy-start.85
  33.4 3.3 copy-start.91
  36.7 2.9 copy-start.82
  39.5 5.2 copy-start.11
  44.7 3.3 copy-start.88
  50.9 4.3 copy-start.88
  58.1 4.3 copy-start.88
  65.2 4.3 copy-start.88
  72.4 3.4 copy-start.94
  90.5 5.0 copy-start.92
  95.6 35.2 %copy-start.67 = (f32[512]{0:T(512)}, f32[512]{0:T(512)S(1)}, u32[]{:S(2)}) copy-start(f32[512]{0:T(512)S(1)} %mul.754) | copy-start | bytes 6148
  95.6 21.0 %copy-start.65 = (f32[512]{0:T(512)S(1)}, f32[512]{0:T(512)}, u32[]{:S(2)}) copy-start(f32[512]{0:T(512)} %param.36) | copy-start | bytes 6148
  115.9 93.4 %copy-start.37 = (f32[1024]{0:T(1024)}, f32[1024]{0:T(1024)S(1)}, u32[]{:S(2)}) copy-start(f32[1024]{0:T(1024)S(1)} %get-tuple-element.585) | copy-start | bytes 12292
  116.6 5.9 copy-start.99
  199.6 6.7 copy-start.16
  199.6 6.7 copy-start.79
  199.6 5.5 copy-start.12
  199.6 5.5 copy-start.21
  209.2 130.1 %reduce-scatter.2.cloned.1.call-start = ((), (), s32[]{:S(2)}) async-start(), calls=%async_computation.1 | async-start | bytes 5242880 | tf_op jit(solution)/shard_map/reduce_scatter | solution.py:152
  214.6 3.3 copy-start.4
  214.6 413.6 %all-gather.3.cloned.1.call-start = ((), (), s32[]{:S(2)}) async-start(), calls=%async_computation.3 | async-start | bytes 20971520 | tf_op jit(solution)/shard_map/all_gather | solution.py:15
  217.9 3.6 copy-start.15
  217.9 3.6 copy-start.30
  217.9 3.6 copy-start.33
  238.4 3.0 copy-start.44
  238.4 3.0 copy-start.50
  238.4 3.3 copy-start.80
  238.4 3.3 copy-start.84
  238.4 3.5 copy-start.40
  238.4 3.5 copy-start.54
  238.4 3.5 copy-start.55
  238.4 3.5 copy-start.56
  252.1 3.0 copy-start.18
  252.1 3.0 copy-start.19
  252.5 3.2 copy-start.8
  252.5 3.8 copy-start.9
  252.5 3.8 copy-start.36
  252.5 3.8 copy-start.68
  256.3 4.1 copy-start.60
  256.3 4.1 copy-start.62
  256.3 4.1 copy-start.64
  268.3 479.4 %all-reduce.34.cloned.1.call-start = ((), (), s32[]{:S(2)}) async-start(), calls=%async_computation.4 | async-start | bytes 14680064 | tf_op jit(solution)/shard_map/psum | solution.py:191
  270.3 3.9 copy-start.27
  279.6 4.2 copy-start.73
  279.6 4.2 copy-start.75
  279.6 4.2 copy-start.77
  289.0 3.4 copy-start.98
  628.2 10.3 %copy-start.46 = (f32[1024]{0:T(1024)S(1)}, f32[1024]{0:T(1024)}, u32[]{:S(2)}) copy-start(f32[1024]{0:T(1024)} %copy-done.45) | copy-start | bytes 12292
  628.2 10.3 %copy-start.52 = (f32[1024]{0:T(1024)S(1)}, f32[1024]{0:T(1024)}, u32[]{:S(2)}) copy-start(f32[1024]{0:T(1024)} %param.24) | copy-start | bytes 12292
  638.5 5.9 copy-start.87
  638.5 33.2 %copy-start.69 = (f32[1024]{0:T(1024)S(1)}, f32[1024]{0:T(1024)}, u32[]{:S(2)}) copy-start(f32[1024]{0:T(1024)} %get-tuple-element.582) | copy-start | bytes 12292
  747.8 3.2 copy-start.25
  (44 other events, 88.5 us)
Sparse Core Ops, SparseCore 0:
  209.3 51.5 all-reduce.31
  263.3 76.0 reduce-scatter.1
  340.9 287.2 all-gather.2
  632.8 114.9 all-reduce.33
